TPU v7x, 128 devices: a whole 4x4x4 slice. The times are simulated.
128 devices in a mesh: alpha: 8 (over x, core), beta: 16 (over z, y).
Axes of the slice: x: 4, y: 4, z: 4, core: 2. Of those that a mesh axis runs over, the one named last changes fastest.
Arguments:
- csf_coef: float32 [42, 98304], P(None, ('alpha', 'beta')), may hold values from -18 to 18
- conf_class: int32 [98304], P(('alpha', 'beta')), may hold values from 0 to 5
- conf_tile: int32 [98304, 1], P(('alpha', 'beta')), may hold values from 0 to 127, as said below
- transforms: float32 [6, 42, 256], replicated, may hold values from -1 to 1
- alpha_targets: int32 [16, 12288], P(None, 'alpha'), may hold values from 0 to 12287, as said below
- alpha_values: bfloat16 [16, 12288], P(None, 'alpha'), may hold values from -1.796875 to 1.796875
- alpha_counts: int32 [12288], P('alpha'), may hold values from 1 to 16, as said below
- beta_targets: int32 [16, 6144], P(None, 'beta'), may hold values from 0 to 6143, as said below
- beta_values: bfloat16 [16, 6144], P(None, 'beta'), may hold values from -1.796875 to 1.796875
- beta_counts: int32 [6144], P('beta'), may hold values from 1 to 16, as said below
- det_diag: float32 [12288, 6144], P('alpha', 'beta'), may hold values from 0.5 to 2
Outputs:
- residual: float32 [42, 98304], P(None, ('alpha', 'beta'))
- residual_rms: float32 [], replicated
Inputs may be any that keep to these rules, and one draw needn't show every extreme that they name: `conf_tile`: among the 768 configurations of one device no tile is named more than 18 times; in every draw some tile is named exactly 18 times by the configurations of every device. `alpha_targets`: in each column the 16 entries are distinct and differ from the column's own string. `beta_targets`: in each column the 16 entries are distinct and differ from the column's own string. `alpha_counts`: some string has exactly 16. `beta_counts`: some string has exactly 16.
All inputs are finite; a program needn't handle non-finite values.
Results may differ from a plain program's by a relative error of at most 0.00075.
The roundings to bfloat16 on the way count: a program that leaves them out, or rounds other values in their place, can miss the bound.
Values may be sent and summed in bfloat16 or wider, within the bound.
No kernel may reach another device: no remote copies, remote signals or barrier semaphores. Data moves between devices by JAX's collectives and lax.ppermute only.
A program may use at most 128 MiB of HBM per device.

v0:
```python
import math

import jax
import jax.numpy as jnp
from jax import lax
from jax.sharding import PartitionSpec as P


def class_forward(coefs, classes, transforms):
    summed = jnp.zeros((coefs.shape[1], transforms.shape[2]), jnp.float32)
    for class_id in range(transforms.shape[0]):
        masked = jnp.where(classes[None, :] == class_id, coefs, jnp.zeros_like(coefs))
        summed = summed + lax.dot_general(
            masked,
            transforms[class_id],
            (((0,), (0,)), ((), ())),
            precision=lax.Precision.HIGHEST,
            preferred_element_type=jnp.float32,
        )
    return summed


def class_backward(values, classes, transforms):
    summed = jnp.zeros((transforms.shape[1], values.shape[0]), jnp.float32)
    for class_id in range(transforms.shape[0]):
        product = lax.dot_general(
            transforms[class_id],
            values,
            (((1,), (1,)), ((), ())),
            precision=lax.Precision.HIGHEST,
            preferred_element_type=jnp.float32,
        )
        summed = summed + jnp.where(classes[None, :] == class_id, product, jnp.zeros_like(product))
    return summed


def bucket_slots(chosen_tiles, buckets):
    onehot = (chosen_tiles[:, None] == jnp.arange(buckets, dtype=jnp.int32)[None, :]).astype(
        jnp.int32
    )
    running = jnp.cumsum(onehot, axis=0) - onehot
    return jnp.sum(onehot * running, axis=1)


def live_weights(values, counts):
    active = jnp.arange(values.shape[0], dtype=jnp.int32)[:, None] < counts[None, :]
    return jnp.where(active, values.astype(jnp.float32), jnp.zeros(values.shape, jnp.float32))


def coupling_block(targets, weights, first_row, block_rows, columns):
    block_targets = lax.dynamic_slice_in_dim(targets, first_row, block_rows, 1)
    block_weights = lax.dynamic_slice_in_dim(weights, first_row, block_rows, 1)
    coupling = jnp.zeros((block_rows, columns.shape[0]), jnp.float32)
    for excitation in range(targets.shape[0]):
        coupling = coupling + jnp.where(
            block_targets[excitation][:, None] == columns[None, :],
            block_weights[excitation][:, None],
            jnp.float32(0.0),
        )
    return coupling.astype(jnp.bfloat16)


def alpha_fold(targets, weights, block_rows, summed, gathered):
    columns = jnp.arange(gathered.shape[0], dtype=jnp.int32)

    def alpha_one_block(block_id):
        coupling = coupling_block(targets, weights, block_id * block_rows, block_rows, columns)
        return jnp.dot(coupling, gathered, preferred_element_type=jnp.float32)

    blocks = lax.map(alpha_one_block, jnp.arange(summed.shape[0] // block_rows, dtype=jnp.int32))
    return blocks.reshape(summed.shape)


def beta_fold(targets, weights, block_rows, summed, gathered):
    columns = jnp.arange(gathered.shape[1], dtype=jnp.int32)

    def beta_one_block(block_id):
        coupling = coupling_block(targets, weights, block_id * block_rows, block_rows, columns)
        return lax.dot_general(
            gathered, coupling, (((1,), (1,)), ((), ())), preferred_element_type=jnp.float32
        )

    blocks = lax.map(beta_one_block, jnp.arange(summed.shape[1] // block_rows, dtype=jnp.int32))
    return jnp.moveaxis(blocks, 0, 1).reshape(summed.shape)


def body(
    csf_coef,
    conf_class,
    conf_tile,
    transforms,
    alpha_targets,
    alpha_values,
    alpha_counts,
    beta_targets,
    beta_values,
    beta_counts,
    det_diag,
):
    nalpha = lax.axis_size("alpha")
    beta_devices = lax.axis_size("beta")
    devices = nalpha * beta_devices
    local_confs = csf_coef.shape[1]
    capacity = 3 * local_confs // devices
    rows_alpha, cols_beta = det_diag.shape
    det_width = transforms.shape[2]
    target_tile = conf_tile[:, 0]
    slot_index = bucket_slots(target_tile, devices)
    det_values = class_forward(csf_coef, conf_class, transforms).astype(jnp.bfloat16)
    outgoing = (
        jnp.zeros((devices, capacity, det_width), jnp.bfloat16)
        .at[target_tile, slot_index]
        .set(det_values)
    )
    arrived = lax.all_to_all(outgoing, ("alpha", "beta"), split_axis=0, concat_axis=0, tiled=True)
    amplitude = arrived.reshape(rows_alpha, cols_beta)
    alpha_weights = live_weights(alpha_values, alpha_counts)
    alpha_term = alpha_fold(
        alpha_targets,
        alpha_weights,
        math.gcd(rows_alpha, 256),
        jnp.zeros((rows_alpha, cols_beta), jnp.float32),
        lax.all_gather(amplitude, "alpha", axis=0, tiled=True),
    )
    beta_weights = live_weights(beta_values, beta_counts)
    beta_term = beta_fold(
        beta_targets,
        beta_weights,
        math.gcd(cols_beta, 256),
        jnp.zeros((rows_alpha, cols_beta), jnp.float32),
        lax.all_gather(amplitude, "beta", axis=1, tiled=True),
    )
    sigma_grid = (alpha_term + beta_term + det_diag * amplitude.astype(jnp.float32)).astype(
        jnp.bfloat16
    )
    returned = lax.all_to_all(
        sigma_grid.reshape(devices, capacity, det_width),
        ("alpha", "beta"),
        split_axis=0,
        concat_axis=0,
        tiled=True,
    )
    sigma_dets = returned[target_tile, slot_index].astype(jnp.float32)
    sigma_csf = class_backward(sigma_dets, conf_class, transforms)
    own_square = jnp.sum(csf_coef * csf_coef)
    own_cross = jnp.sum(csf_coef * sigma_csf)
    total_entries = csf_coef.shape[0] * local_confs * devices
    square_sum, cross_sum = lax.psum((own_square, own_cross), ("alpha", "beta"))
    rayleigh = cross_sum / square_sum
    residual = sigma_csf - rayleigh * csf_coef
    residual_square = lax.psum(jnp.sum(residual * residual), ("alpha", "beta"))
    residual_rms = jnp.sqrt(residual_square / total_entries)
    return (residual, residual_rms)


def solution(mesh):
    placed = (
        P(None, ("alpha", "beta")),
        P(("alpha", "beta")),
        P(("alpha", "beta"), None),
        P(),
        P(None, "alpha"),
        P(None, "alpha"),
        P("alpha"),
        P(None, "beta"),
        P(None, "beta"),
        P("beta"),
        P("alpha", "beta"),
    )
    return jax.shard_map(
        body,
        mesh=mesh,
        in_specs=placed,
        out_specs=(P(None, ("alpha", "beta")), P()),
        check_vma=False,
    )
```

profile of v0, /device:TPU:1, one launch (start us, length us, event | category | flops | bytes accessed | tf_op | source)
XLA Modules:
  0.0 629.4 jit_solution(12536454217057345708)
XLA Ops:
  7.2 0.8 broadcast_compare_fusion
  8.0 0.7 reduce
  9.5 1.3 fusion.143
  10.8 1.6 fusion.97
  12.5 0.8 convolution_add_fusion.4
  13.3 0.8 convolution_add_fusion.3
  14.2 0.8 convolution_add_fusion.2
  15.0 0.8 convolution_add_fusion.1
  15.9 0.9 fusion.80
  16.9 37.6 %scatter_fusion = bf16[128,18,256]{2,0,1:T(8,128)(2,1)S(1)} fusion(bf16[128,18,256]{2,0,1:T(8,128)(2,1)S(1)} %broadcast_in_dim.410, s32[768]{0:T(1024)S(1)} %get-tuple-element.263, bf16[768,256]{1,0:T(8,128)(2,1)S(1)} %fusion.80), kind=kCustom, calls=%fused_computation.1 | custom fusion | bytes 1185792 | tf_op jit(solution)/shard_map/scatter | solution.py:113
  54.5 0.7 copy.27
  55.2 35.2 %all_to_all.10 = bf16[128,18,256]{2,1,0:T(8,128)(2,1)S(1)} all-to-all(bf16[128,18,256]{2,1,0:T(8,128)(2,1)S(1)} %copy.27), channel_id=1, replica_groups=mesh['alpha'=8,'beta'=16] {'alpha','beta'}, dimensions={0} | all-to-all | bytes 2359296 | tf_op jit(solution)/shard_map/all_to_all | solution.py:115
  90.4 1.7 reshape.130
  92.2 0.7 all-gather.5.cloned.1.call-update
  93.5 49.5 %all-gather.3.cloned.1.call-done = bf16[12288,384]{1,0:T(8,128)(2,1)} async-done(((bf16[1536,384]{1,0:T(8,128)(2,1)}), bf16[12288,384]{1,0:T(8,128)(2,1)}) %all-gather.3.cloned.1.call-update) | async-done | bytes 9437200 | tf_op jit(solution)/shard_map/all_gather | solution.py:123
  143.1 233.3 %while.24 = (s32[]{:T(128)}, f32[6,256,384]{2,1,0:T(8,128)}, s32[6]{0:T(128)S(1)}, s32[16,1536]{1,0:T(8,128)}, f32[16,1536]{1,0:T(8,128)S(1)}, /*index=5*/bf16[1...) while((s32[]{:T(128)}, f32[6,256,384]{2,1,0:T(8,128)}, ...), condition=%wide.region_5.6_spmd.clone.clone, body=%wide.region_4.5_spmd.clone.clone.sunk | while | flops 2566914048 | bytes 9929803 | solution.py:70
  162.0 0.7 dynamic_slice.34
  163.5 1.4 constant_dynamic-slice_fusion.7
  164.9 31.6 %fusion.159 = f32[6,256,384]{2,1,0:T(8,128)} fusion(f32[6,256,384]{2,1,0:T(8,128)} %get-tuple-element.666, s32[]{:T(128)} %get-tuple-element.665, bf16[12288,384]{1,0:T(8,128)(2,1)} %get-tuple-element.695, f32[256]{0:T(256)S(1)} %bitcast.268, s32[256]{0:T(256)S(1)} %bitcast.284, f32[256]{0:T(256)S(1)} %bitcast.254, s32[256]{0:T(256)S(1)} %bitcast.270, ...), kind=kOutput, calls=%fused_computation.56.clone.1 | convolution fusion | flops 2566914048 | bytes 9863680 | tf_op jit(solution)/shard_map/while/body/eval_jaxpr/dot_general | solution.py:68
  198.0 1.4 constant_dynamic-slice_fusion.7
  199.4 31.8 %fusion.159 = f32[6,256,384]{2,1,0:T(8,128)} fusion(f32[6,256,384]{2,1,0:T(8,128)} %get-tuple-element.666, s32[]{:T(128)} %get-tuple-element.665, bf16[12288,384]{1,0:T(8,128)(2,1)} %get-tuple-element.695, f32[256]{0:T(256)S(1)} %bitcast.268, s32[256]{0:T(256)S(1)} %bitcast.284, f32[256]{0:T(256)S(1)} %bitcast.254, s32[256]{0:T(256)S(1)} %bitcast.270, ...), kind=kOutput, calls=%fused_computation.56.clone.1 | convolution fusion | flops 2566914048 | bytes 9863680 | tf_op jit(solution)/shard_map/while/body/eval_jaxpr/dot_general | solution.py:68
  232.6 1.4 constant_dynamic-slice_fusion.7
  234.0 31.4 %fusion.159 = f32[6,256,384]{2,1,0:T(8,128)} fusion(f32[6,256,384]{2,1,0:T(8,128)} %get-tuple-element.666, s32[]{:T(128)} %get-tuple-element.665, bf16[12288,384]{1,0:T(8,128)(2,1)} %get-tuple-element.695, f32[256]{0:T(256)S(1)} %bitcast.268, s32[256]{0:T(256)S(1)} %bitcast.284, f32[256]{0:T(256)S(1)} %bitcast.254, s32[256]{0:T(256)S(1)} %bitcast.270, ...), kind=kOutput, calls=%fused_computation.56.clone.1 | convolution fusion | flops 2566914048 | bytes 9863680 | tf_op jit(solution)/shard_map/while/body/eval_jaxpr/dot_general | solution.py:68
  267.0 1.4 constant_dynamic-slice_fusion.7
  268.4 31.4 %fusion.159 = f32[6,256,384]{2,1,0:T(8,128)} fusion(f32[6,256,384]{2,1,0:T(8,128)} %get-tuple-element.666, s32[]{:T(128)} %get-tuple-element.665, bf16[12288,384]{1,0:T(8,128)(2,1)} %get-tuple-element.695, f32[256]{0:T(256)S(1)} %bitcast.268, s32[256]{0:T(256)S(1)} %bitcast.284, f32[256]{0:T(256)S(1)} %bitcast.254, s32[256]{0:T(256)S(1)} %bitcast.270, ...), kind=kOutput, calls=%fused_computation.56.clone.1 | convolution fusion | flops 2566914048 | bytes 9863680 | tf_op jit(solution)/shard_map/while/body/eval_jaxpr/dot_general | solution.py:68
  301.3 1.2 constant_dynamic-slice_fusion.7
  302.5 31.5 %fusion.159 = f32[6,256,384]{2,1,0:T(8,128)} fusion(f32[6,256,384]{2,1,0:T(8,128)} %get-tuple-element.666, s32[]{:T(128)} %get-tuple-element.665, bf16[12288,384]{1,0:T(8,128)(2,1)} %get-tuple-element.695, f32[256]{0:T(256)S(1)} %bitcast.268, s32[256]{0:T(256)S(1)} %bitcast.284, f32[256]{0:T(256)S(1)} %bitcast.254, s32[256]{0:T(256)S(1)} %bitcast.270, ...), kind=kOutput, calls=%fused_computation.56.clone.1 | convolution fusion | flops 2566914048 | bytes 9863680 | tf_op jit(solution)/shard_map/while/body/eval_jaxpr/dot_general | solution.py:68
  335.4 1.2 constant_dynamic-slice_fusion.7
  336.6 31.4 %fusion.159 = f32[6,256,384]{2,1,0:T(8,128)} fusion(f32[6,256,384]{2,1,0:T(8,128)} %get-tuple-element.666, s32[]{:T(128)} %get-tuple-element.665, bf16[12288,384]{1,0:T(8,128)(2,1)} %get-tuple-element.695, f32[256]{0:T(256)S(1)} %bitcast.268, s32[256]{0:T(256)S(1)} %bitcast.284, f32[256]{0:T(256)S(1)} %bitcast.254, s32[256]{0:T(256)S(1)} %bitcast.270, ...), kind=kOutput, calls=%fused_computation.56.clone.1 | convolution fusion | flops 2566914048 | bytes 9863680 | tf_op jit(solution)/shard_map/while/body/eval_jaxpr/dot_general | solution.py:68
  376.5 66.2 %while.25 = (s32[]{:T(128)}, f32[3,1536,128]{1,2,0:T(8,128)}, s32[3]{0:T(128)S(1)}, s32[16,384]{1,0:T(8,128)}, f32[16,384]{1,0:T(8,128)}, /*index=5*/bf16[1536,6...) while((s32[]{:T(128)}, f32[3,1536,128]{1,2,0:T(8,128)}, ...), condition=%wide.region_7.8_spmd.clone.clone, body=%wide.region_6.7_spmd.clone.clone.sunk | while | flops 2453667840 | bytes 19711052 | solution.py:83
  377.7 1.1 fusion.161
  378.9 1.1 fusion.162
  380.0 18.5 %fusion.163 = f32[3,1536,128]{1,2,0:T(8,128)} fusion(f32[3,1536,128]{1,2,0:T(8,128)} %get-tuple-element.591, s32[]{:T(128)} %get-tuple-element.590, bf16[1536,6144]{1,0:T(8,128)(2,1)} %get-tuple-element.620, f32[128]{0:T(128)S(1)} %get-tuple-element.533, s32[128]{0:T(128)S(1)} %get-tuple-element.534, f32[128]{0:T(128)S(1)} %get-tuple-element.535, ...), kind=kOutput, calls=%fused_computation.78.clone.1 | convolution fusion | flops 2453667840 | bytes 19677696 | tf_op jit(solution)/shard_map/while/body/eval_jaxpr/dot_general | solution.py:79
  399.8 1.1 fusion.161
  400.9 1.1 fusion.162
  402.1 18.5 %fusion.163 = f32[3,1536,128]{1,2,0:T(8,128)} fusion(f32[3,1536,128]{1,2,0:T(8,128)} %get-tuple-element.591, s32[]{:T(128)} %get-tuple-element.590, bf16[1536,6144]{1,0:T(8,128)(2,1)} %get-tuple-element.620, f32[128]{0:T(128)S(1)} %get-tuple-element.533, s32[128]{0:T(128)S(1)} %get-tuple-element.534, f32[128]{0:T(128)S(1)} %get-tuple-element.535, ...), kind=kOutput, calls=%fused_computation.78.clone.1 | convolution fusion | flops 2453667840 | bytes 19677696 | tf_op jit(solution)/shard_map/while/body/eval_jaxpr/dot_general | solution.py:79
  421.9 1.1 fusion.161
  423.0 1.1 fusion.162
  424.1 18.5 %fusion.163 = f32[3,1536,128]{1,2,0:T(8,128)} fusion(f32[3,1536,128]{1,2,0:T(8,128)} %get-tuple-element.591, s32[]{:T(128)} %get-tuple-element.590, bf16[1536,6144]{1,0:T(8,128)(2,1)} %get-tuple-element.620, f32[128]{0:T(128)S(1)} %get-tuple-element.533, s32[128]{0:T(128)S(1)} %get-tuple-element.534, f32[128]{0:T(128)S(1)} %get-tuple-element.535, ...), kind=kOutput, calls=%fused_computation.78.clone.1 | convolution fusion | flops 2453667840 | bytes 19677696 | tf_op jit(solution)/shard_map/while/body/eval_jaxpr/dot_general | solution.py:79
  442.7 2.1 copy.28
  444.8 3.8 fusion.79
  448.6 2.5 reshape.133
  451.2 31.9 %all_to_all.11 = bf16[128,18,256]{2,1,0:T(8,128)(2,1)S(1)} all-to-all(bf16[128,18,256]{2,1,0:T(8,128)(2,1)S(1)} %reshape.133), channel_id=1, replica_groups=mesh['alpha'=8,'beta'=16] {'alpha','beta'}, dimensions={0} | all-to-all | bytes 2359296 | tf_op jit(solution)/shard_map/all_to_all | solution.py:136
  483.4 4.2 gather_fusion
  490.2 1.1 multiply_reduce_fusion.1
  491.3 63.8 %all-reduce = (f32[]{:T(128)}, f32[]{:T(128)}) all-reduce(f32[]{:T(128)} %get-tuple-element.261, f32[]{:T(128)} %get-tuple-element.260), channel_id=1, replica_groups=mesh['alpha'=8,'beta'=16] {'alpha','beta'}, use_global_device_ids=true, to_apply=%region_9.10 | all-reduce | flops 2 | bytes 16 | tf_op jit(solution)/shard_map/psum | solution.py:148
  556.4 1.3 multiply_reduce_fusion
  557.7 62.8 %psum.23 = f32[]{:T(128)} all-reduce(f32[]{:T(128)} %get-tuple-element.290), channel_id=1, replica_groups=mesh['alpha'=8,'beta'=16] {'alpha','beta'}, use_global_device_ids=true, to_apply=%region_13.14 | all-reduce | flops 1 | bytes 8 | tf_op jit(solution)/shard_map/psum | solution.py:151
  (82 shorter events, 10.5 us)
Async XLA Ops:
  7.2 3.7 copy-start.2
  7.2 5.3 copy-start.4
  7.2 135.9 %all-gather.3.cloned.1.call-start = ((), (), s32[]{:S(2)}) async-start(), calls=%async_computation.2 | async-start | bytes 10616832 | tf_op jit(solution)/shard_map/all_gather | solution.py:123
  8.0 6.2 copy-start.14
  8.0 6.2 copy-start.16
  8.0 6.2 copy-start.18
  8.0 6.2 copy-start.12
  8.0 7.0 %copy-start.10 = (pred[768]{0:T(1024)(128)(4,1)}, pred[768]{0:T(1024)(128)(4,1)S(1)}, u32[]{:S(2)}) copy-start(pred[768]{0:T(1024)(128)(4,1)S(1)} %get-tuple-element.361) | copy-start | bytes 2308
  8.0 7.8 %copy-start.8 = (pred[768]{0:T(1024)(128)(4,1)}, pred[768]{0:T(1024)(128)(4,1)S(1)}, u32[]{:S(2)}) copy-start(pred[768]{0:T(1024)(128)(4,1)S(1)} %get-tuple-element.356) | copy-start | bytes 2308
  90.4 2.5 copy-start.7
  90.4 2.5 copy-start.21
  90.4 3.1 copy-start.6
  90.4 3.1 copy-start.20
  92.1 284.3 %all-gather.5.cloned.1.call-start = ((), (), s32[]{:S(2)}) async-start(), calls=%async_computation.3 | async-start | bytes 20054016 | tf_op jit(solution)/shard_map/all_gather | solution.py:131
  442.7 2.1 copy-start.1
  451.1 32.2 %copy-start = (s32[768]{0:T(1024)S(1)}, s32[768]{0:T(1024)}, u32[]{:S(2)}) copy-start(s32[768]{0:T(1024)} %get-tuple-element.262) | copy-start | bytes 9220
  483.1 4.5 copy-start.5
  483.1 4.6 copy-start.19
  483.1 5.1 copy-start.17
  483.3 5.3 copy-start.15
  483.3 5.8 copy-start.13
  483.4 6.3 copy-start.11
  483.4 6.8 %copy-start.3 = (f32[42,768]{1,0:T(8,128)S(1)}, f32[42,768]{1,0:T(8,128)}, u32[]{:S(2)}) copy-start(f32[42,768]{1,0:T(8,128)} %param.15) | copy-start | bytes 387076
  483.4 6.8 %copy-start.9 = (pred[768]{0:T(1024)(128)(4,1)S(1)}, pred[768]{0:T(1024)(128)(4,1)}, u32[]{:S(2)}) copy-start(pred[768]{0:T(1024)(128)(4,1)} %copy-done.8) | copy-start | bytes 2308
Sparse Core Ops, SparseCore 0:
  92.2 50.7 all-gather.2
  145.2 129.1 all-gather.4
where the time goes:
time: 637 us; the launch traced here: 629 us
  matrix products  254 us (40%)
  blocking collectives  194 us (30%)
  local copies, waits for them, and re-layouts  70.8 us (11%)
  waiting for transfers between devices  50.3 us (8%)
  loops' own time  33.5 us (5%)
  between operations  17.9 us (3%)
  other arithmetic  9.02 us (1%)
    dot_general x6, matrix products, alpha_one_block(): return jnp.dot(coupling, gathered, preferred_element_type=jnp.float32)  189 us
    psum x1, blocking collectives, body(): square_sum, cross_sum = lax.psum((own_square, own_cross), ('alpha', 'beta'))  63.8 us
    psum x1, blocking collectives, body(): residual_square = lax.psum(jnp.sum(residual * residual), ('alpha', 'beta'))  62.8 us
    dot_general x3, matrix products, beta_one_block(): lax.dot_general(gathered, coupling, (((1,), (1,)), ((), ())), preferred_e...  55.6 us
    all_gather x1, waiting for transfers between devices, body(): lax.all_gather(amplitude, 'alpha', axis=0, tiled=True)  49.5 us
    scatter x2, local copies, waits for them, and re-layouts, body(): outgoing = jnp.zeros((devices, capacity, det_width), jnp.bfloat16).at[tar...  38.3 us
    all_to_all x1, blocking collectives, body(): lax.all_to_all(outgoing, ('alpha', 'beta'), split_axis=0, concat_axis=0,...  35.2 us
    all_to_all x1, blocking collectives, body(): lax.all_to_all(sigma_grid.reshape(devices, capacity, det_width), ('alpha'...  31.9 us
  transfers between devices with their start and end apart: 2, of which 1 were waited for; matrix products, arithmetic and copies ran while one was open for 32% of the time, Pallas kernels for 0%

commit v1 on v0

v1 whole, which is shorter than its diff:
```python
import functools

import jax
import jax.numpy as jnp
from jax import lax
from jax.experimental import pallas as pl
from jax.experimental.pallas import tpu as pltpu
from jax.sharding import PartitionSpec as P

F32 = jnp.float32
BF16 = jnp.bfloat16
HIGH = lax.Precision.HIGHEST
BOTH = ("alpha", "beta")
PAD = 8
VMEM_LIMIT = 60 * 1024 * 1024


def masked_coefs(coef, classes, classes_n, width):
    parts = []
    for c in range(classes_n):
        parts.append(jnp.where(classes == c, coef, jnp.zeros_like(coef)))
    return jnp.concatenate(parts, axis=0)


def pack_kernel(capacity, coef_ref, class_ref, tile_ref, tr_ref, out_ref, key_ref, inter_ref):
    confs = coef_ref.shape[1]
    ncls = tr_ref.shape[0] // coef_ref.shape[0]
    devices = confs * 3 // capacity
    masked = masked_coefs(coef_ref[...], class_ref[...], ncls, confs)
    dets = lax.dot_general(
        masked, tr_ref[...], (((0,), (0,)), ((), ())), precision=HIGH, preferred_element_type=F32
    ).astype(BF16)
    tile = tile_ref[...]
    hit = lax.broadcasted_iota(jnp.int32, (devices, confs), 0) == tile
    before = lax.broadcasted_iota(jnp.int32, (confs, confs), 0) < lax.broadcasted_iota(
        jnp.int32, (confs, confs), 1
    )
    counts = jnp.dot(
        hit.astype(F32).astype(BF16), before.astype(F32).astype(BF16), preferred_element_type=F32
    )
    slot = jnp.sum(jnp.where(hit, counts, 0.0), axis=0, keepdims=True).astype(jnp.int32)
    key = tile * capacity + slot
    key_ref[...] = key
    rows = devices * capacity
    block = 256
    for b in range(rows // block):
        onehot = (
            (lax.broadcasted_iota(jnp.int32, (block, confs), 0) + b * block == key)
            .astype(F32)
            .astype(BF16)
        )
        picked = jnp.dot(onehot, dets, preferred_element_type=F32)
        for h in range(2):
            inter_ref[pl.ds(h, block, stride=2), :] = picked[:, h * 128 : (h + 1) * 128]
        out_ref[pl.ds(b * 2 * block, 2 * block), :] = inter_ref[...].astype(BF16)


def pack(coef48, classes, tiles, tr, capacity):
    confs = coef48.shape[1]
    rows = 2 * 3 * confs
    return pl.pallas_call(
        functools.partial(pack_kernel, capacity),
        out_shape=(
            jax.ShapeDtypeStruct((rows, 128), BF16),
            jax.ShapeDtypeStruct((1, confs), jnp.int32),
        ),
        scratch_shapes=[pltpu.VMEM((512, 128), F32)],
        compiler_params=pltpu.CompilerParams(vmem_limit_bytes=VMEM_LIMIT),
        name="pack",
    )(coef48, classes, tiles, tr)


def beta_kernel(x_ref, tgt_ref, w_ref, out_ref, table_ref, wt_ref, acc_ref, stage_ref):
    blocks = x_ref.shape[0]
    rows = x_ref.shape[1]
    lanes = rows // 3

    @pl.when(pl.program_id(0) == 0)
    def _():
        def build(j, carry):
            stage_ref[...] = x_ref[j].astype(F32)
            for ct in range(3):
                piece = stage_ref[pl.ds(ct, lanes, stride=3), :]
                piece = jnp.concatenate([piece, jnp.zeros((128 - lanes, 128), F32)], axis=0)
                start = pl.multiple_of((j * 3 + ct) * 128 + PAD, 8)
                table_ref[pl.ds(start, 128), :] = piece.T
            return carry

        lax.fori_loop(0, blocks, build, 0)

    sub = lax.broadcasted_iota(jnp.int32, (8, 128), 0)
    for ct in range(3):
        wt_ref[...] = jnp.concatenate(
            [w_ref[0, pl.ds(ct, 16, stride=3), :], jnp.zeros((112, 128), F32)], axis=0
        ).T

        def group(g, carry):
            first = g * 8
            w8 = wt_ref[pl.ds(pl.multiple_of(first, 8), 8), :]
            acc = jnp.zeros((8, 128), F32)
            for e in range(16):
                got = None
                for s in range(8):
                    t = tgt_ref[0, e * 3 + ct, first + s]
                    win = table_ref[pl.ds(t + (PAD - s), 8), :]
                    got = win if s == 0 else jnp.where(sub == s, win, got)
                acc = acc + got * w8[:, e : e + 1]
            acc_ref[pl.ds(pl.multiple_of(first, 8), 8), :] = acc
            return carry

        lax.fori_loop(0, 16, group, 0)
        out_ref[0, pl.ds(ct, lanes, stride=3), :] = acc_ref[...].T[:lanes]


def beta_term(x2, targets, weights):
    blocks, rows, _ = x2.shape
    cols = blocks * 384
    return pl.pallas_call(
        beta_kernel,
        out_shape=jax.ShapeDtypeStruct((blocks, rows, 128), F32),
        grid=(blocks,),
        in_specs=[
            pl.BlockSpec((blocks, rows, 128), lambda j: (0, 0, 0)),
            pl.BlockSpec((1, 48, 128), lambda j: (j, 0, 0), memory_space=pltpu.SMEM),
            pl.BlockSpec((1, 48, 128), lambda j: (j, 0, 0)),
        ],
        out_specs=pl.BlockSpec((1, rows, 128), lambda j: (j, 0, 0)),
        scratch_shapes=[
            pltpu.VMEM((cols + 2 * PAD, 128), F32),
            pltpu.VMEM((128, 128), F32),
            pltpu.VMEM((128, 128), F32),
            pltpu.VMEM((rows, 128), F32),
        ],
        compiler_params=pltpu.CompilerParams(vmem_limit_bytes=VMEM_LIMIT),
        cost_estimate=pl.CostEstimate(
            flops=2 * cols * 16 * 1024, bytes_accessed=8 * 2**20, transcendentals=0
        ),
        name="beta_term",
    )(x2, targets, weights)


def alpha_kernel(
    nsend, own_ref, tbl_hbm, tgt_ref, w_ref, diag_ref, out_ref, table_ref, dpiece_ref, buf_ref, sem
):
    chunk = buf_ref.shape[1]
    total = tbl_hbm.shape[0]
    n = total // chunk

    def fetch(k, slot):
        return pltpu.make_async_copy(
            tbl_hbm.at[pl.ds(pl.multiple_of(k * chunk, 16), chunk), :],
            buf_ref.at[slot],
            sem.at[slot],
        )

    fetch(0, 0).start()
    rows = diag_ref.shape[0]

    def interleave(k, carry):
        base = pl.multiple_of(k * 8, 8)
        for ct in range(3):
            dpiece_ref[pl.ds(base * 3 + ct, 8, stride=3), :] = diag_ref[
                pl.ds(base, 8), ct * 128 : (ct + 1) * 128
            ]
        return carry

    lax.fori_loop(0, rows // 8, interleave, 0)

    def load(k, carry):
        slot = lax.rem(k, 2)

        @pl.when(k + 1 < n)
        def _():
            fetch(k + 1, 1 - slot).start()

        fetch(k, slot).wait()
        table_ref[pl.ds(pl.multiple_of(k * chunk, 8), chunk), :] = buf_ref[slot].astype(F32)
        return carry

    lax.fori_loop(0, n, load, 0)
    per = rows // nsend
    own = own_ref[0]
    halves = nsend // 16

    def sender(k, carry):
        beta_s = k // halves
        alpha_s = k - beta_s * halves
        nat = (alpha_s * 16 + beta_s) * per
        pos = k * per
        for r in range(per):
            a = nat + r
            o = (pos + r) * 3
            acc = jnp.zeros((8, 128), F32)
            for e in range(16):
                acc = acc + table_ref[pl.ds(tgt_ref[e, a], 8), :] * w_ref[e, a]
            acc = acc + dpiece_ref[pl.ds(a * 3, 8), :] * table_ref[pl.ds(own + o, 8), :]
            out_ref[pl.ds(o, 8), :] = acc
        return carry

    lax.fori_loop(0, nsend, sender, 0)


def alpha_term(own, table, targets, weights, diag, nsend):
    rows = diag.shape[0]
    total = table.shape[0]
    chunk = total // 16
    return pl.pallas_call(
        functools.partial(alpha_kernel, nsend),
        out_shape=jax.ShapeDtypeStruct((rows * 3 + PAD, 128), F32),
        in_specs=[
            pl.BlockSpec(memory_space=pltpu.SMEM),
            pl.BlockSpec(memory_space=pl.ANY),
            pl.BlockSpec(memory_space=pltpu.SMEM),
            pl.BlockSpec(memory_space=pltpu.SMEM),
            pl.BlockSpec(memory_space=pltpu.VMEM),
        ],
        out_specs=pl.BlockSpec(memory_space=pltpu.VMEM),
        scratch_shapes=[
            pltpu.VMEM((total + PAD, 128), F32),
            pltpu.VMEM((rows * 3 + PAD, 128), F32),
            pltpu.VMEM((2, chunk, 128), BF16),
            pltpu.SemaphoreType.DMA((2,)),
        ],
        compiler_params=pltpu.CompilerParams(vmem_limit_bytes=VMEM_LIMIT),
        name="alpha_term",
    )(own, table, targets, weights, diag)


def unpack_kernel(
    r_ref, key_ref, class_ref, coef_ref, tr_ref, sigma_ref, part_ref, stage_ref, half_ref
):
    rows2 = r_ref.shape[0]
    rows = rows2 // 2
    confs = key_ref.shape[1]
    width = coef_ref.shape[0]
    ncls = tr_ref.shape[0] // width
    stage_ref[...] = r_ref[...].astype(F32)
    for h in range(2):
        half_ref[:, h * 128 : (h + 1) * 128] = stage_ref[pl.ds(h, rows, stride=2), :].astype(BF16)
    key = key_ref[...]
    block = 256
    dets = jnp.zeros((256, confs), F32)
    for b in range(rows // block):
        onehot = (
            (lax.broadcasted_iota(jnp.int32, (block, confs), 0) + b * block == key)
            .astype(F32)
            .astype(BF16)
        )
        dets = dets + lax.dot_general(
            half_ref[pl.ds(b * block, block), :],
            onehot,
            (((0,), (0,)), ((), ())),
            preferred_element_type=F32,
        )
    products = jnp.dot(tr_ref[...], dets, precision=HIGH, preferred_element_type=F32)
    sigma = jnp.zeros((width, confs), F32)
    for c in range(ncls):
        sigma = sigma + jnp.where(class_ref[...] == c, products[c * width : (c + 1) * width], 0.0)
    coef = coef_ref[...]
    sigma_ref[...] = sigma
    square = jnp.sum(jnp.sum(coef * coef, axis=1, keepdims=True), axis=0, keepdims=True)
    cross = jnp.sum(jnp.sum(coef * sigma, axis=1, keepdims=True), axis=0, keepdims=True)
    ratio = jnp.where(square > 0.0, cross / jnp.where(square > 0.0, square, 1.0), 0.0)
    rest = sigma - ratio * coef
    rho = jnp.sum(jnp.sum(rest * rest, axis=1, keepdims=True), axis=0, keepdims=True)
    lane = lax.broadcasted_iota(jnp.int32, (1, 128), 1)
    part_ref[...] = jnp.where(
        lane == 0,
        square,
        jnp.where(lane == 1, cross, jnp.where(lane == 2, rho, jnp.where(lane == 3, ratio, 0.0))),
    )


def unpack(returned, key, classes, coef48, tr):
    confs = coef48.shape[1]
    return pl.pallas_call(
        unpack_kernel,
        out_shape=(
            jax.ShapeDtypeStruct(coef48.shape, F32),
            jax.ShapeDtypeStruct((1, 128), F32),
        ),
        scratch_shapes=[
            pltpu.VMEM(returned.shape, F32),
            pltpu.VMEM((returned.shape[0] // 2, 256), BF16),
        ],
        compiler_params=pltpu.CompilerParams(vmem_limit_bytes=VMEM_LIMIT),
        name="unpack",
    )(returned, key, classes, coef48, tr)


def exchange(x, axes):
    return lax.all_to_all(x, axes, split_axis=0, concat_axis=0, tiled=True)


def body(
    csf_coef,
    conf_class,
    conf_tile,
    transforms,
    alpha_targets,
    alpha_values,
    alpha_counts,
    beta_targets,
    beta_values,
    beta_counts,
    det_diag,
):
    nalpha = lax.axis_size("alpha")
    nbeta = lax.axis_size("beta")
    devices = nalpha * nbeta
    ncsf, confs = csf_coef.shape
    capacity = 3 * confs // devices
    rows_alpha, cols_beta = det_diag.shape
    classes_n, _, width = transforms.shape
    exc = alpha_targets.shape[0]
    pieces = capacity * width // 128
    per = pieces * 128 // cols_beta
    csf_pad = -ncsf % 8
    coef48 = jnp.pad(csf_coef, ((0, csf_pad), (0, 0)))
    tr = jnp.pad(transforms, ((0, 0), (0, csf_pad), (0, 0))).reshape(-1, width)
    classes = conf_class[None, :]
    tiles = conf_tile[:, 0][None, :]

    slots = jnp.arange(exc, dtype=jnp.int32)[:, None]
    live_beta = jnp.where(slots < beta_counts[None, :], beta_values, jnp.zeros_like(beta_values))
    lists = jnp.concatenate(
        [
            (beta_targets // 128).astype(BF16).reshape(-1, 128),
            (beta_targets % 128).astype(BF16).reshape(-1, 128),
            live_beta.reshape(-1, 128),
        ],
        axis=0,
    )

    outgoing, key = pack(coef48, classes, tiles, tr, capacity)
    slab = exchange(outgoing.reshape(nalpha, nbeta * pieces, 128), "alpha")
    x2 = (
        slab.reshape(nalpha, nbeta, pieces, 128)
        .transpose(1, 0, 2, 3)
        .reshape(nbeta, nalpha * pieces, 128)
    )
    sent = jnp.concatenate(
        [x2, jnp.broadcast_to(lists[None], (nbeta,) + lists.shape)], axis=1
    )
    got = exchange(sent, "beta")
    body_rows = nalpha * pieces
    tile = got[:, :body_rows].reshape(-1, 128)
    lrows = lists.shape[0] // 3
    high = got[:, body_rows : body_rows + lrows].astype(jnp.int32)
    low = got[:, body_rows + lrows : body_rows + 2 * lrows].astype(jnp.int32)
    btargets = high * 128 + low
    bweights = got[:, body_rows + 2 * lrows :].astype(F32)

    table = lax.all_gather(tile, "alpha", axis=0, tiled=True)
    beta_slab = beta_term(x2, btargets, bweights)

    owner = alpha_targets // rows_alpha
    inner = alpha_targets % rows_alpha
    sender = inner // per
    row = inner % per
    place = ((sender % nbeta) * nalpha + sender // nbeta) * per + row
    atargets = (owner * rows_alpha + place) * (cols_beta // 128)
    aweights = jnp.where(slots < alpha_counts[None, :], alpha_values.astype(F32), 0.0)
    own = (lax.axis_index("alpha") * (rows_alpha * cols_beta // 128)).astype(jnp.int32)[None]
    partial = alpha_term(own, table, atargets, aweights, det_diag, devices)
    partial = partial[: rows_alpha * 3].reshape(nbeta, body_rows, 128)
    passed = exchange(partial, "beta")
    sigma_slab = (
        (passed + beta_slab)
        .astype(BF16)
        .reshape(nbeta, nalpha, pieces, 128)
        .transpose(1, 0, 2, 3)
        .reshape(nalpha, nbeta * pieces, 128)
    )
    returned = exchange(sigma_slab, "alpha").reshape(-1, 128)
    sigma48, part = unpack(returned, key, classes, coef48, tr)
    parts = exchange(jnp.broadcast_to(part[None], (devices, 1, 128)), BOTH)[:, 0]
    square = parts[:, 0]
    rayleigh = jnp.sum(parts[:, 1]) / jnp.sum(square)
    shift = rayleigh - parts[:, 3]
    residual_square = jnp.sum(parts[:, 2] + shift * shift * square)
    residual = sigma48[:ncsf] - rayleigh * csf_coef
    residual_rms = jnp.sqrt(residual_square / (ncsf * confs * devices))
    return (residual, residual_rms)


def solution(mesh):
    placed = (
        P(None, BOTH),
        P(BOTH),
        P(BOTH, None),
        P(),
        P(None, "alpha"),
        P(None, "alpha"),
        P("alpha"),
        P(None, "beta"),
        P(None, "beta"),
        P("beta"),
        P("alpha", "beta"),
    )
    return jax.shard_map(
        body,
        mesh=mesh,
        in_specs=placed,
        out_specs=(P(None, BOTH), P()),
        check_vma=False,
    )
```

time: 637 us -> 434 us (0.68)
  matrix products: 254 us -> 0 us
  Pallas kernels: 0 us -> 242 us
  blocking collectives: 194 us -> 69.2 us
  local copies, waits for them, and re-layouts: 70.8 us -> 14.9 us
  loops' own time: 33.5 us -> 0 us
  waiting for transfers between devices: 50.3 us -> 66.5 us
  starting transfers between devices: 0.08 us -> 12.5 us
    dot_general x21 -> x0, matrix products: 254 us -> none  [the longest x6 189 us: alpha_one_block(): return jnp.dot(coupling, gathered, preferred_element_type=jnp.float32)]
    pallas_call x0 -> x4, Pallas kernels: none -> 242 us  [the longest x1 182 us: beta_term(): pl.pallas_call(beta_kernel, out_shape=jax.ShapeDtypeStruct((blocks, rows,...]
    psum x2 -> x0, blocking collectives: 127 us -> none  [the longest x1 63.8 us: body(): square_sum, cross_sum = lax.psum((own_square, own_cross), ('alpha', 'beta'))]
    scatter x2 -> x0, local copies, waits for them, and re-layouts: 38.3 us -> none  [body(): outgoing = jnp.zeros((devices, capacity, det_width), jnp.bfloat16).at[tar...]
    another operation x2 -> x0, loops' own time: 33.5 us -> none  [the longest x1 31.5 us: alpha_fold(): lax.map(alpha_one_block, jnp.arange(summed.shape[0] // block_rows, dtype=...]
    all_to_all x0 -> x2, waiting for transfers between devices: none -> 16.2 us  [exchange(): return lax.all_to_all(x, axes, split_axis=0, concat_axis=0, tiled=True)]
    all_to_all x0 -> x2, starting transfers between devices: none -> 12.5 us  [exchange(): return lax.all_to_all(x, axes, split_axis=0, concat_axis=0, tiled=True)]
    all_to_all x2 -> x3, blocking collectives: 67.2 us -> 69.2 us  [exchange(): return lax.all_to_all(x, axes, split_axis=0, concat_axis=0, tiled=True)]
  transfers between devices with their start and end apart: 2 -> 3, of which waited for: 1 -> 2; matrix products, arithmetic and copies ran while one was open for 32% -> 1% of each run, Pallas kernels for 0% -> 42%
where the time goes in v1:
time: 434 us; the launch traced here: 433 us
  Pallas kernels  242 us (56%)
  blocking collectives  69.2 us (16%)
  waiting for transfers between devices  66.5 us (15%)
  between operations  17.4 us (4%)
  local copies, waits for them, and re-layouts  14.9 us (3%)
  starting transfers between devices  12.5 us (3%)
  other arithmetic  10.1 us (2%)
    pallas_call x1, Pallas kernels, beta_term(): pl.pallas_call(beta_kernel, out_shape=jax.ShapeDtypeStruct((blocks, rows,...  182 us
    all_to_all x3, blocking collectives, exchange(): return lax.all_to_all(x, axes, split_axis=0, concat_axis=0, tiled=True)  69.2 us
    all_gather x1, waiting for transfers between devices, body(): table = lax.all_gather(tile, 'alpha', axis=0, tiled=True)  50.2 us
    pallas_call x1, Pallas kernels, alpha_term(): pl.pallas_call(functools.partial(alpha_kernel, nsend), out_shape=jax.Shap...  48.9 us
    all_to_all x2, waiting for transfers between devices, exchange(): return lax.all_to_all(x, axes, split_axis=0, concat_axis=0, tiled=True)  16.2 us
    all_to_all x2, starting transfers between devices, exchange(): return lax.all_to_all(x, axes, split_axis=0, concat_axis=0, tiled=True)  12.5 us
  transfers between devices with their start and end apart: 3, of which 2 were waited for; matrix products, arithmetic and copies ran while one was open for 1% of the time, Pallas kernels for 42%

profile of v1, /device:TPU:1, one launch (start us, length us, event | category | flops | bytes accessed | tf_op | source)
XLA Modules:
  0.0 432.6 jit_solution(5510490390184656504)
XLA Ops:
  7.2 1.3 broadcast_in_dim.31.class_ref
  8.4 1.6 pad.8.coef_ref
  10.0 1.7 pad.9
  11.8 6.7 %pack.1 = (bf16[4608,128]{1,0:T(8,128)(2,1)}, s32[1,768]{1,0:T(1,128)}) custom-call(f32[48,768]{1,0:T(8,128)} %pad.8.coef_ref, s32[1,768]{1,0:T(1,128)} %broadcast_in_dim.31.class_ref, s32[1,768]{1,0:T(1,128)} %bitcast.28, f32[288,256]{1,0:T(8,128)} %bitcast.23), custom_call_target="tpu_custom_call" | custom-call | tf_op jit(solution)/shard_map/pack/pallas_call | solution.py:61
  18.4 5.8 %all-to-all-start = ((bf16[8,576,128]{2,1,0:T(8,128)(2,1)}), bf16[8,576,128]{2,1,0:T(8,128)(2,1)S(1)}, u32[]{:S(2)}, u32[]{:S(2)}) async-start(bf16[8,576,128]{2,1,0:T(8,128)(2,1)} %bitcast.25), calls=%async_computation | async-start | bytes 2359296 | tf_op jit(solution)/shard_map/all_to_all | solution.py:292
  24.2 0.0 all-gather.2.cloned.1.call-start
  24.2 0.0 copy-done.6
  24.2 0.0 copy-done.8
  24.3 0.0 copy-done.5
  24.4 16.2 %all-to-all-done = bf16[8,576,128]{2,1,0:T(8,128)(2,1)S(1)} async-done(((bf16[8,576,128]{2,1,0:T(8,128)(2,1)}), bf16[8,576,128]{2,1,0:T(8,128)(2,1)S(1)}, u32[]{:S(2)}, u32[]{:S(2)}) %all-to-all-start) | async-done | bytes 1179680 | tf_op jit(solution)/shard_map/all_to_all | solution.py:292
  40.6 0.8 copy.45
  41.4 0.5 copy.46
  41.8 0.3 copy.47.x_ref
  42.1 0.0 copy-start
  42.2 0.1 broadcast_in_dim.33
  42.2 0.1 pad_maximum_fusion
  42.4 0.8 copy-done
  43.2 31.1 %all_to_all.25 = bf16[16,432,128]{2,1,0:T(8,128)(2,1)S(1)} all-to-all(bf16[16,432,128]{2,1,0:T(8,128)(2,1)S(1)} %pad_maximum_fusion), channel_id=1, replica_groups=mesh['alpha'=8,'beta'=16] {'beta'}, dimensions={0} | all-to-all | bytes 3538944 | tf_op jit(solution)/shard_map/all_to_all | solution.py:292
  74.3 1.3 copy-done.1
  75.6 1.1 slice.40
  76.7 0.0 all-gather.2.cloned.1.call-update
  76.7 0.0 copy-done.4
  76.7 0.0 copy-done.7
  76.7 0.7 convert_select_fusion.w_ref
  77.4 0.0 copy-done.3
  77.4 0.9 fusion.2.tgt_ref
  78.3 50.2 %all-gather.2.cloned.1.call-done.tbl_hbm = bf16[36864,128]{1,0:T(8,128)(2,1)} async-done(((bf16[4608,128]{1,0:T(8,128)(2,1)}), bf16[36864,128]{1,0:T(8,128)(2,1)}) %all-gather.2.cloned.1.call-update) | async-done | bytes 9437200 | tf_op jit(solution)/shard_map/all_gather | solution.py:354
  128.6 48.9 %alpha_term.1 = f32[4616,128]{1,0:T(8,128)} custom-call(s32[1]{0:T(128)} %bitcast.own_ref, bf16[36864,128]{1,0:T(8,128)(2,1)} %all-gather.2.cloned.1.call-done.tbl_hbm, s32[16,1536]{1,0:T(8,128)} %fusion.2.tgt_ref, f32[16,1536]{1,0:T(8,128)} %convert_select_fusion.w_ref, f32[1536,384]{1,0:T(8,128)} %diag_ref.1), custom_call_target="tpu_custom_call" | custom-call | tf_op jit(solution)/shard_map/alpha_term/pallas_call | solution.py:207
  177.4 3.2 slice.41
  180.7 6.7 %all-to-all-start.2 = ((f32[16,288,128]{2,1,0:T(8,128)}), f32[16,288,128]{2,1,0:T(8,128)S(1)}, u32[]{:S(2)}, u32[]{:S(2)}) async-start(f32[16,288,128]{2,1,0:T(8,128)} %bitcast.8), calls=%async_computation.2 | async-start | bytes 4718592 | tf_op jit(solution)/shard_map/all_to_all | solution.py:292
  187.4 1.9 convert_add_fusion.tgt_ref
  189.3 1.7 slice_convert_fusion.w_ref
  191.0 181.7 %beta_term.1 = f32[16,288,128]{2,1,0:T(8,128)} custom-call(bf16[16,288,128]{2,1,0:T(8,128)(2,1)} %copy-done, s32[16,48,128]{2,1,0:T(8,128)} %convert_add_fusion.tgt_ref, f32[16,48,128]{2,1,0:T(8,128)} %slice_convert_fusion.w_ref), custom_call_target="tpu_custom_call" | custom-call | flops 201326592 | bytes 8388608 | tf_op jit(solution)/shard_map/beta_term/pallas_call | solution.py:118
  372.7 0.0 all-to-all-done.2
  372.7 1.9 add_convert_fusion
  374.6 0.5 copy.49
  375.1 0.8 copy.50
  375.8 0.2 copy.51
  376.0 0.0 copy-start.2
  376.0 20.3 %all_to_all.26 = bf16[8,576,128]{2,1,0:T(8,128)(2,1)} all-to-all(bf16[8,576,128]{2,1,0:T(8,128)(2,1)S(1)} %copy.51), channel_id=1, replica_groups=mesh['alpha'=8,'beta'=16] {'alpha'}, dimensions={0} | all-to-all | bytes 2359296 | tf_op jit(solution)/shard_map/all_to_all | solution.py:292
  396.3 4.9 %unpack.1 = (f32[48,768]{1,0:T(8,128)}, f32[1,128]{1,0:T(1,128)}) custom-call(bf16[4608,128]{1,0:T(8,128)(2,1)} %bitcast.18, s32[1,768]{1,0:T(1,128)} %get-tuple-element.7.key_ref, s32[1,768]{1,0:T(1,128)} %broadcast_in_dim.31.class_ref, f32[48,768]{1,0:T(8,128)} %pad.8.coef_ref, f32[288,256]{1,0:T(8,128)} %bitcast.24), custom_call_target="tpu_custom_call" | custom-call | tf_op jit(solution)/shard_map/unpack/pallas_call | solution.py:276
  401.2 0.7 broadcast_in_dim.36
  401.9 17.8 %all_to_all.27 = f32[128,1,128]{2,1,0:T(1,128)S(1)} all-to-all(f32[128,1,128]{2,1,0:T(1,128)S(1)} %broadcast_in_dim.36), channel_id=1, replica_groups=mesh['alpha'=8,'beta'=16] {'alpha','beta'}, dimensions={0} | all-to-all | bytes 131072 | tf_op jit(solution)/shard_map/all_to_all | solution.py:292
  419.7 0.1 copy.52
  419.8 0.6 slice_reduce_fusion.1
  421.8 0.6 fusion.21
  423.1 0.0 copy-done.2
  423.1 1.6 multiply_subtract_fusion
  (13 shorter events, 0.1 us)
Async XLA Ops:
  10.0 14.2 %copy-start.6 = (bf16[16,384]{1,0:T(8,128)(2,1)S(1)}, bf16[16,384]{1,0:T(8,128)(2,1)}, u32[]{:S(2)}) copy-start(bf16[16,384]{1,0:T(8,128)(2,1)} %param.19) | copy-start | bytes 36868
  10.0 14.2 %copy-start.8 = (s32[384]{0:T(512)S(1)}, s32[384]{0:T(512)}, u32[]{:S(2)}) copy-start(s32[384]{0:T(512)} %param.20) | copy-start | bytes 4612
  10.0 14.3 %copy-start.5 = (s32[16,384]{1,0:T(8,128)S(1)}, s32[16,384]{1,0:T(8,128)}, u32[]{:S(2)}) copy-start(s32[16,384]{1,0:T(8,128)} %param.18) | copy-start | bytes 73732
  18.4 22.2 %all-to-all-start = ((bf16[8,576,128]{2,1,0:T(8,128)(2,1)}), bf16[8,576,128]{2,1,0:T(8,128)(2,1)S(1)}, u32[]{:S(2)}, u32[]{:S(2)}) async-start(bf16[8,576,128]{2,1,0:T(8,128)(2,1)} %bitcast.25), calls=%async_computation | async-start | bytes 2359296 | tf_op jit(solution)/shard_map/all_to_all | solution.py:292
  24.2 104.3 %all-gather.2.cloned.1.call-start = ((), (), s32[]{:S(2)}) async-start(), calls=%async_computation.5 | async-start | bytes 10616832 | tf_op jit(solution)/shard_map/all_gather | solution.py:354
  42.1 1.0 copy-start
  74.3 1.3 copy-start.1
  75.6 1.1 copy-start.4
  75.6 1.1 copy-start.7
  75.6 1.8 copy-start.3
  180.7 192.0 %all-to-all-start.2 = ((f32[16,288,128]{2,1,0:T(8,128)}), f32[16,288,128]{2,1,0:T(8,128)S(1)}, u32[]{:S(2)}, u32[]{:S(2)}) async-start(f32[16,288,128]{2,1,0:T(8,128)} %bitcast.8), calls=%async_computation.2 | async-start | bytes 4718592 | tf_op jit(solution)/shard_map/all_to_all | solution.py:292
  376.0 47.1 %copy-start.2 = (f32[42,768]{1,0:T(8,128)S(1)}, f32[42,768]{1,0:T(8,128)}, u32[]{:S(2)}) copy-start(f32[42,768]{1,0:T(8,128)} %param.11) | copy-start | bytes 387076
Sparse Core Ops, SparseCore 0:
  76.8 51.6 all-gather.1
